TPU v7x, 512 devices: a whole 4x4x16 slice. The times are simulated.
512 devices in a mesh: delay: 64 (over y, x, z_hi, core), row: 8 (over z_lo).
Axes of the slice: x: 4, y: 4, z: 16 (z_hi: 2, z_lo: 8; z = z_hi * 8 + z_lo), core: 2. Of those that a mesh axis runs over, the one named last changes fastest.
Arguments:
- excite: bfloat16 [1, 4096, 128], P(None, 'row'), may hold values from -6 to 6
- present_inverse: bfloat16 [32, 128, 128], P('row'), may hold values from -0.5 to 0.5
- retarded: bfloat16 [64, 32, 16, 128, 128], P('delay', 'row'), may hold values from -0.125 to 0.125
- columns: int32 [64, 32, 16], P('delay', 'row'), may hold values from 0 to 31, as said below
- future_in: float32 [64, 4096, 128], P('delay', 'row'), may hold values from -6 to 6
Outputs:
- currents: bfloat16 [1, 4096, 128], P(None, 'row')
- future_out: float32 [64, 4096, 128], P('delay', 'row')
Inputs may be any that keep to these rules, and one draw needn't show every extreme that they name: `columns`: each block row at each delay names 16 different column blocks.
All inputs are finite; a program needn't handle non-finite values.
Results may differ from a plain program's by a relative error of at most 0.0052.
Values may be sent and summed in bfloat16 or wider, within the bound.
A program may use at most 64 MiB of HBM per device.

v0:
```python
import jax
import jax.numpy as jnp
from jax import lax
from jax.sharding import PartitionSpec as P

BLK = 128


def from_root(value, axis, source):
    kept = jnp.where(lax.axis_index(axis) == source, value, 0).astype(value.dtype)
    return lax.psum(kept, axis)


def from_behind(shard, axis, by):
    devices = lax.axis_size(axis)
    pairs = [(i, i + by) for i in range(devices) if 0 <= i + by < devices]
    return lax.ppermute(shard, axis, pairs)


def per_device(excite, present_inverse, retarded, columns, future_in):
    rows = future_in.shape[1]
    width = future_in.shape[2]
    row_blocks = rows // BLK
    future = future_in[0]
    weights = retarded[0]
    indices = columns[0]
    right_side = (excite[0].astype(jnp.float32) - future).astype(jnp.bfloat16)
    stacked = right_side.reshape(row_blocks, BLK, width)
    solved = lax.dot_general(
        present_inverse, stacked, (((2,), (1,)), ((0,), (0,))), preferred_element_type=jnp.float32
    )
    own_rows = solved.astype(jnp.bfloat16).reshape(rows, width)
    collected = lax.all_gather(own_rows, "row", axis=0, tiled=True)
    whole = from_root(collected, "delay", 0)
    present = lax.dynamic_slice_in_dim(whole, lax.axis_index("row") * rows, rows, 0)
    history = [present]
    shifted = from_behind(future.astype(jnp.bfloat16), "delay", -1).astype(future.dtype)
    total_blocks = whole.shape[0] // BLK
    picked = whole.reshape(total_blocks, BLK, width)[indices]
    added = lax.dot_general(
        weights, picked, (((1, 3), (1, 2)), ((0,), (0,))), preferred_element_type=jnp.float32
    )
    future = shifted + added.reshape(rows, width)
    return (jnp.stack(history), future[None])


def solution(mesh):
    return jax.shard_map(
        per_device,
        mesh=mesh,
        in_specs=(
            P(None, "row", None),
            P("row", None, None),
            P("delay", "row", None, None, None),
            P("delay", "row", None),
            P("delay", "row", None),
        ),
        out_specs=(P(None, "row", None), P("delay", "row", None)),
        check_vma=False,
    )
```

profile of v0, /device:TPU:1, one launch (start us, length us, event | category | flops | bytes accessed | tf_op | source)
XLA Modules:
  0.0 1178.6 jit_solution(8119319604677655539)
XLA Ops:
  7.2 0.0 copy-start
  7.2 0.0 copy-start.1
  7.2 0.0 all-gather.2.cloned.1.call-start
  7.2 1.2 convert_bitcast_fusion
  8.5 1.7 convolution_convert_fusion
  10.2 0.0 all-gather.2.cloned.1.call-update
  10.2 0.0 all-reduce.2.cloned.1.call-start
  10.3 66.4 %all-gather.2.cloned.1.call-done = bf16[4096,128]{1,0:T(8,128)(2,1)} async-done(((bf16[512,128]{1,0:T(8,128)(2,1)}), bf16[4096,128]{1,0:T(8,128)(2,1)}) %all-gather.2.cloned.1.call-update) | async-done | bytes 1048592 | tf_op jit(solution)/shard_map/all_gather | solution.py:33
  76.7 1.0 broadcast_select_fusion
  77.7 0.0 all-reduce.2.cloned.1.call-update
  77.7 10.6 collective-permute-start
  88.3 0.0 copy-done.1
  88.3 0.1 reshape.53
  88.4 1075.3 %all-reduce.2.cloned.1.call-done = bf16[4096,128]{1,0:T(8,128)(2,1)} async-done(((bf16[4096,128]{1,0:T(8,128)(2,1)}), bf16[4096,128]{1,0:T(8,128)(2,1)}) %all-reduce.2.cloned.1.call-update) | async-done | bytes 1048592 | tf_op jit(solution)/shard_map/psum | solution.py:11
  1163.7 3.4 gather_fusion
  1167.1 0.0 copy-done
  1167.1 2.3 fusion
  1169.4 1.6 dynamic-slice_bitcast_fusion
  1171.0 0.0 collective-permute-done
  1171.0 0.7 bitcast_add_fusion
  (2 shorter events, 0.0 us)
Async XLA Ops:
  7.2 1160.0 %copy-start = (bf16[1,4,16,128,128]{4,3,2,1,0:T(8,128)(2,1)S(1)}, bf16[1,4,16,128,128]{4,3,2,1,0:T(8,128)(2,1)}, u32[]{:S(2)}) copy-start(bf16[1,4,16,128,128]{4,3,2,1,0:T(8,128)(2,1)} %param.7) | copy-start | bytes 6291460
  7.2 81.1 %copy-start.1 = (s32[1,4,16]{2,1,0:T(4,128)S(1)}, s32[1,4,16]{2,1,0:T(4,128)}, u32[]{:S(2)}) copy-start(s32[1,4,16]{2,1,0:T(4,128)} %param.8) | copy-start | bytes 772
  7.2 69.5 %all-gather.2.cloned.1.call-start = ((), (), s32[]{:S(2)}) async-start(), calls=%async_computation | async-start | bytes 1179648 | tf_op jit(solution)/shard_map/all_gather | solution.py:33
  10.2 1153.5 %all-reduce.2.cloned.1.call-start = ((), (), s32[]{:S(2)}) async-start(), calls=%async_computation.1 | async-start | bytes 2097152 | tf_op jit(solution)/shard_map/psum | solution.py:11
  77.7 1093.3 %collective-permute-start = (bf16[512,128]{1,0:T(8,128)(2,1)S(1)}, bf16[512,128]{1,0:T(8,128)(2,1)S(1)}, u32[]{:S(2)}, u32[]{:S(2)}) collective-permute-start(bf16[512,128]{1,0:T(8,128)(2,1)S(1)} %get-tuple-element.2), channel_id=1, source_target_pairs={{8,0},{16,8},{24,16},{32,24},{40,32},{48,40},{56,48},{64,56},{72,6... | collective-permute-start | bytes 393224 | tf_op jit(solution)/shard_map/ppermute | solution.py:17
Sparse Core Ops, SparseCore 0:
  10.7 65.9 all-gather.1
  79.5 1084.1 all-reduce.1
where the time goes:
time: 1180 us
  waiting for transfers between devices  1140 us (97%)
  between operations  14.1 us (1%)
    psum x1, waiting for transfers between devices, from_root(): return lax.psum(kept, axis)  1080 us
    all_gather x1, waiting for transfers between devices, per_device(): collected = lax.all_gather(own_rows, 'row', axis=0, tiled=True)  66.4 us
  transfers between devices with their start and end apart: 3, of which 2 were waited for; matrix products, arithmetic and copies ran while one was open for 1% of the time, Pallas kernels for 0%

commit v1 on v0

v1 whole, which is shorter than its diff:
```python
import functools

import jax
import jax.numpy as jnp
from jax import lax
from jax.experimental import pallas as pl
from jax.experimental.pallas import tpu as pltpu
from jax.sharding import PartitionSpec as P

MESH = pl.DeviceIdType.MESH
BLK = 128
ROWS = 512
RB = 4
NNZ = 16
WID = 128
LINE = 16
FAR = (8, 7, 9, 6, 10, 5, 11, 4, 12, 3, 13, 2, 14, 1, 15)
HOPS = (1, 3, 2)
ORDER = sorted(range(1, 32), key=lambda p: -(min((p // 4) % 4, 4 - (p // 4) % 4) + min(p % 4, 4 - p % 4)))


def gather_kernel(
    excite, inverse, future, whole, shift,
    ex_v, inv_v, fut_v, cast_v, sol_v, relay,
    load_sem, p1_send, p1_recv, rl_send, rl_recv, p2_send, p2_recv, p0_send,
    a_send, a_recv, b_send, b_recv, c_send, c_recv, sh_send, sh_recv,
):
    d = lax.axis_index("delay")
    r = lax.axis_index("row")
    core = d % 2
    zh = (d // 2) % 2
    x = (d // 4) % 4
    y = d // 16
    z = zh * 8 + r
    step_a = 4 + 12 * core
    step_b = 16 - 12 * core
    a = x * (1 - core) + y * core
    b = y * (1 - core) + x * core
    base = d - zh * 2
    mine = core * 16 + b * 4 + a
    near = zh == 0
    source = d == 0
    helper = d == 1

    def at_z(first, k):
        zz = k % LINE
        return (first + (zz // 8) * 2, zz % 8)

    def peer_a(k):
        return (d + ((a + k) % 4 - a) * step_a, r)

    def peer_b(k):
        return (d + ((b + k) % 4 - b) * step_b, r)

    partner = (d + 1 - 2 * core, r)

    barrier = pltpu.get_barrier_semaphore()

    def greet(device):
        pl.semaphore_signal(barrier, inc=1, device_id=device, device_id_type=MESH)

    @pl.when(near & (d != 0))
    def _():
        greet((0, r))

    on_root_line = base == 0
    line_sender = jnp.where(on_root_line, 1, base)
    for s in range(8):
        @pl.when((jnp.logical_not(near)) | (r != s))
        def _(s=s):
            greet((line_sender, s))
    @pl.when(helper)
    def _():
        greet((0, r))
    for k in HOPS:
        greet(peer_a(k))
        greet(peer_b(k))
    greet(partner)

    @pl.when(d < 63)
    def _():
        greet((d + 1, r))

    fut_in = pltpu.make_async_copy(future.at[0], fut_v, load_sem.at[0])
    fut_in.start()

    @pl.when(source)
    def _():
        ex_in = pltpu.make_async_copy(excite.at[0], ex_v, load_sem.at[1])
        inv_in = pltpu.make_async_copy(inverse, inv_v, load_sem.at[2])
        ex_in.start()
        inv_in.start()
        fut_in.wait()
        ex_in.wait()
        inv_in.wait()
        right = (ex_v[...].astype(jnp.float32) - fut_v[...]).astype(jnp.bfloat16)
        for k in range(RB):
            got = jnp.dot(inv_v[k], right[k * BLK:(k + 1) * BLK], preferred_element_type=jnp.float32)
            sol_v[pl.ds(k * 8, 8)] = got.astype(jnp.bfloat16).reshape(8, 16, WID)
        whole[0, r] = sol_v[0]
        pl.semaphore_wait(barrier, 31 + 7 + 1)
        for p in ORDER + [0]:
            pc, pb, pa = p // 16, (p // 4) % 4, p % 4
            px, py = (pa, pb) if pc == 0 else (pb, pa)
            if p == 0:
                continue
            pltpu.make_async_remote_copy(
                sol_v.at[p], whole.at[p, r], p1_send.at[p], p1_recv,
                device_id=((py * 4 + px) * 4 + pc, r), device_id_type=MESH,
            ).start()
        pltpu.make_async_remote_copy(
            sol_v.at[0], relay, rl_send, rl_recv, device_id=(1, r), device_id_type=MESH
        ).start()

    @pl.when(d > 0)
    def _():
        fut_in.wait()
        cast_v[...] = fut_v[...].astype(jnp.bfloat16)

    def shift_copy():
        return pltpu.make_async_remote_copy(
            cast_v, shift, sh_send, sh_recv, device_id=(d - 1, r), device_id_type=MESH
        )

    def line_copy(k):
        return pltpu.make_async_remote_copy(
            whole.at[mine, r], whole.at[mine, r], p2_send.at[k], p2_recv.at[r],
            device_id=at_z(base, z + k), device_id_type=MESH,
        )

    def root_copy(k):
        return pltpu.make_async_remote_copy(
            relay, whole.at[0, r], p0_send.at[k], p2_recv.at[r],
            device_id=at_z(0, z + k), device_id_type=MESH,
        )

    @pl.when(near & helper)
    def _():
        pl.semaphore_wait(barrier, 15 + 15 + 7 + 1)
        shift_copy().start()

    @pl.when(near & (d > 1))
    def _():
        pl.semaphore_wait(barrier, 15 + 7 + 1)

    @pl.when(jnp.logical_not(near))
    def _():
        pl.semaphore_wait(barrier, 7 + 1)
        shift_copy().start()

    @pl.when(near & (d > 1) & (core == 1))
    def _():
        shift_copy().start()

    @pl.when(near & (d > 0))
    def _():
        pltpu.make_async_remote_copy(
            sol_v.at[0], whole.at[mine, r], p1_send.at[0], p1_recv, device_id=(0, r), device_id_type=MESH
        ).wait_recv()
        for k in FAR:
            line_copy(k).start()

    @pl.when(helper)
    def _():
        pltpu.make_async_remote_copy(
            sol_v.at[0], relay, rl_send, rl_recv, device_id=(1, r), device_id_type=MESH
        ).wait_recv()
        for k in FAR:
            root_copy(k).start()

    @pl.when(near & (d > 1) & (core == 0))
    def _():
        shift_copy().start()

    for s in range(8):
        @pl.when((jnp.logical_not(near)) | (r != s))
        def _(s=s):
            pltpu.make_async_remote_copy(
                relay, whole.at[mine, s], p0_send.at[0], p2_recv.at[s], device_id=(0, r), device_id_type=MESH
            ).wait_recv()

    def slab(k, m):
        return core * 16 + ((b + 4 - m) % 4) * 4 + (a + 4 - k) % 4

    def other_slab(k, m):
        return (1 - core) * 16 + ((a + 4 - m) % 4) * 4 + (b + 4 - k) % 4

    def copy_a(k):
        return pltpu.make_async_remote_copy(
            whole.at[mine], whole.at[mine], a_send.at[k], a_recv.at[k],
            device_id=peer_a(k), device_id_type=MESH,
        )

    def copy_b(k, m):
        part = slab(k, 0)
        return pltpu.make_async_remote_copy(
            whole.at[part], whole.at[part], b_send.at[k, m], b_recv.at[k, m],
            device_id=peer_b(m), device_id_type=MESH,
        )

    def copy_c(k, m):
        part = slab(k, m)
        return pltpu.make_async_remote_copy(
            whole.at[part], whole.at[part], c_send.at[k, m], c_recv.at[k, m],
            device_id=partner, device_id_type=MESH,
        )

    def got(part, sem):
        pltpu.make_async_remote_copy(
            whole.at[part], whole.at[part], c_send.at[0, 0], sem, device_id=partner, device_id_type=MESH
        ).wait_recv()

    for k in HOPS:
        copy_a(k).start()
    for m in HOPS:
        copy_b(0, m).start()
    copy_c(0, 0).start()
    for k in HOPS:
        got(slab(k, 0), a_recv.at[k])
        for m in HOPS:
            copy_b(k, m).start()
        copy_c(k, 0).start()
    for k in (0,) + HOPS:
        for m in HOPS:
            got(slab(k, m), b_recv.at[k, m])
            copy_c(k, m).start()
    for k in (0,) + HOPS:
        for m in (0,) + HOPS:
            got(other_slab(k, m), c_recv.at[k, m])

    @pl.when(d < 63)
    def _():
        shift_copy().wait_recv()

    @pl.when(d == 63)
    def _():
        shift[...] = jnp.zeros_like(shift)

    @pl.when(source)
    def _():
        for p in ORDER:
            pltpu.make_async_remote_copy(
                sol_v.at[p], whole.at[p, r], p1_send.at[p], p1_recv, device_id=partner, device_id_type=MESH
            ).wait_send()
        pltpu.make_async_remote_copy(
            sol_v.at[0], relay, rl_send, rl_recv, device_id=partner, device_id_type=MESH
        ).wait_send()

    @pl.when(d > 0)
    def _():
        shift_copy().wait_send()

    @pl.when(near & (d > 0))
    def _():
        for k in FAR:
            line_copy(k).wait_send()

    @pl.when(helper)
    def _():
        for k in FAR:
            root_copy(k).wait_send()

    for k in HOPS:
        copy_a(k).wait_send()
    for k in (0,) + HOPS:
        for m in HOPS:
            copy_b(k, m).wait_send()
    for k in (0,) + HOPS:
        for m in (0,) + HOPS:
            copy_c(k, m).wait_send()


def apply_kernel(row, columns, whole, weights, shift, currents, out):
    r = row[0]
    currents[0] = whole[:, r].reshape(ROWS, WID)
    for i in range(RB):
        left = jnp.concatenate([weights[0, i, k] for k in range(NNZ)], axis=1)
        picked = []
        for k in range(NNZ):
            j = columns[0, i, k]
            quarter = whole[pl.ds((j % 4) * 8, 8), j // 4]
            picked.append(quarter.reshape(BLK, WID))
        right = jnp.concatenate(picked, axis=0)
        total = jnp.dot(left, right, preferred_element_type=jnp.float32)
        rows = pl.ds(i * BLK, BLK)
        out[0, rows] = total + shift[rows].astype(jnp.float32)


def per_device(excite, present_inverse, retarded, columns, future_in):
    vmem = pl.BlockSpec(memory_space=pltpu.VMEM)
    smem = pl.BlockSpec(memory_space=pltpu.SMEM)
    hbm = pl.BlockSpec(memory_space=pl.ANY)
    dma = pltpu.SemaphoreType.DMA
    whole, shift = pl.pallas_call(
        gather_kernel,
        out_shape=(
            jax.ShapeDtypeStruct((32, 8, 16, WID), jnp.bfloat16),
            jax.ShapeDtypeStruct((ROWS, WID), jnp.bfloat16),
        ),
        in_specs=[hbm, hbm, hbm],
        out_specs=(vmem, vmem),
        scratch_shapes=[
            pltpu.VMEM((ROWS, WID), jnp.bfloat16),
            pltpu.VMEM((RB, BLK, BLK), jnp.bfloat16),
            pltpu.VMEM((ROWS, WID), jnp.float32),
            pltpu.VMEM((ROWS, WID), jnp.bfloat16),
            pltpu.VMEM((32, 16, WID), jnp.bfloat16),
            pltpu.VMEM((16, WID), jnp.bfloat16),
            dma((3,)), dma((32,)), dma, dma, dma, dma((16,)), dma((8,)), dma((16,)),
            dma((4,)), dma((4,)), dma((4, 4)), dma((4, 4)), dma((4, 4)), dma((4, 4)), dma, dma,
        ],
        compiler_params=pltpu.CompilerParams(collective_id=0, has_side_effects=True),
        name="gather",
    )(excite, present_inverse, future_in)
    row = lax.axis_index("row").astype(jnp.int32).reshape(1)
    return pl.pallas_call(
        apply_kernel,
        out_shape=(
            jax.ShapeDtypeStruct((1, ROWS, WID), jnp.bfloat16),
            jax.ShapeDtypeStruct((1, ROWS, WID), jnp.float32),
        ),
        in_specs=[smem, smem, vmem, vmem, vmem],
        out_specs=(vmem, vmem),
        name="apply",
    )(row, columns, whole, retarded, shift)


def solution(mesh):
    return jax.shard_map(
        per_device,
        mesh=mesh,
        in_specs=(
            P(None, "row", None),
            P("row", None, None),
            P("delay", "row", None, None, None),
            P("delay", "row", None),
            P("delay", "row", None),
        ),
        out_specs=(P(None, "row", None), P("delay", "row", None)),
        check_vma=False,
    )
```

time: 1180 us -> 45.5 us (0.04)
  waiting for transfers between devices: 1140 us -> 0 us
  Pallas kernels: 0 us -> 44.7 us
  between operations: 14.1 us -> 0.64 us
    psum x1 -> x0, waiting for transfers between devices: 1080 us -> none  [from_root(): return lax.psum(kept, axis)]
    all_gather x1 -> x0, waiting for transfers between devices: 66.4 us -> none  [per_device(): collected = lax.all_gather(own_rows, 'row', axis=0, tiled=True)]
    pallas_call x0 -> x2, Pallas kernels: none -> 44.7 us  [the longest x1 41.4 us: per_device(): pl.pallas_call(gather_kernel, out_shape=(jax.ShapeDtypeStruct((32, 8, 16,...]
  transfers between devices with their start and end apart: 3 -> 0, of which waited for: 2 -> 0; matrix products, arithmetic and copies ran while one was open for 1% -> 0% of each run, Pallas kernels for 0% -> 0%
where the time goes in v1:
time: 45.5 us; the launch traced here: 45.4 us
  Pallas kernels  44.7 us (98%)
  between operations  0.64 us (1%)
    pallas_call x1, Pallas kernels, per_device(): pl.pallas_call(gather_kernel, out_shape=(jax.ShapeDtypeStruct((32, 8, 16,...  41.4 us
    pallas_call x1, Pallas kernels, per_device(): pl.pallas_call(apply_kernel, out_shape=(jax.ShapeDtypeStruct((1, ROWS, WI...  3.36 us

profile of v1, /device:TPU:1, one launch (start us, length us, event | category | flops | bytes accessed | tf_op | source)
XLA Modules:
  0.0 45.4 jit_solution(7070127032315457316)
XLA Ops:
  0.6 41.4 %gather.1 = (bf16[32,8,16,128]{3,2,1,0:T(8,128)(2,1)}, bf16[512,128]{1,0:T(8,128)(2,1)}) custom-call(bf16[1,512,128]{2,1,0:T(8,128)(2,1)} %excite.1, bf16[4,128,128]{2,1,0:T(8,128)(2,1)} %inverse.1, f32[1,512,128]{2,1,0:T(8,128)} %future.1), custom_call_target="tpu_custom_call" | custom-call | tf_op jit(solution)/shard_map/gather/pallas_call | solution.py:294
  42.0 3.4 %apply.1 = (bf16[1,512,128]{2,1,0:T(8,128)(2,1)}, f32[1,512,128]{2,1,0:T(8,128)}) custom-call(s32[1]{0:T(128)} %bitcast.row, s32[1,4,16]{2,1,0:T(4,128)} %columns.1, bf16[32,8,16,128]{3,2,1,0:T(8,128)(2,1)} %get-tuple-element.4.whole, bf16[1,4,16,128,128]{4,3,2,1,0:T(8,128)(2,1)} %weights.1, bf16[512,128]{1,0:T(8,128)(2,1)} %get-tuple-element.5.shift), custom_call_target="tpu_custom_call" | custom-call | tf_op jit(solution)/shard_map/apply/pallas_call | solution.py:316

commit v2 on v0

v2 whole, which is shorter than its diff:
```python
import jax
import jax.numpy as jnp
from jax import lax
from jax.experimental import pallas as pl
from jax.experimental.pallas import tpu as pltpu
from jax.sharding import PartitionSpec as P

MESH = pl.DeviceIdType.MESH
BLK = 128
ROWS = 512
RB = 4
NNZ = 16
WID = 128
HOPS = (1, 3, 2)
REACH = 4


def step_kernel(
    excite, inverse, weights, columns, future, currents, out,
    ex_v, inv_v, w_v, col_s, fut_v, cast_v, shift_v, half_v, src_v, row_v, whole,
    load_sem, half_send, half_recv, one_send, one_recv, few_send, few_recv,
    line_send, line_recv, fwd_send, ready, ready_shift,
    a_send, a_recv, b_send, b_recv, c_send, c_recv, sh_send, sh_recv,
):
    d = lax.axis_index("delay")
    r = lax.axis_index("row")
    core = d % 2
    zh = (d // 2) % 2
    x = (d // 4) % 4
    y = d // 16
    z = zh * 8 + r
    step_a = 4 + 12 * core
    step_b = 16 - 12 * core
    a = x * (1 - core) + y * core
    b = y * (1 - core) + x * core
    base = d - zh * 2
    mine = core * 16 + b * 4 + a
    near = zh == 0
    far = zh == 1
    root = (x + y + zh) == 0
    source = d == 0
    partner = (d + 1 - 2 * core, r)

    def rank_of(line):
        return jnp.where(line < 8, line, 23 - line)

    rank = rank_of(z)

    def wrapped(k):
        return (z + k + 16) % 16

    def at_z(k):
        n = wrapped(k)
        return (base + (n // 8) * 2, n % 8)

    def later(k):
        return rank_of(wrapped(k)) > rank

    def peer_a(k):
        return (d + ((a + k) % 4 - a) * step_a, r)

    def peer_b(k):
        return (d + ((b + k) % 4 - b) * step_b, r)

    def remote(src, dst, send, recv, device):
        return pltpu.make_async_remote_copy(src, dst, send, recv, device_id=device, device_id_type=MESH)

    barrier = pltpu.get_barrier_semaphore()

    def greet(device):
        pl.semaphore_signal(barrier, inc=1, device_id=device, device_id_type=MESH)

    fut_in = pltpu.make_async_copy(future.at[0], fut_v, load_sem.at[0])
    fut_in.start()

    for k in HOPS:
        greet(peer_a(k))
        greet(peer_b(k))
    greet(partner)
    greeted = 7
    steps = [s * k for k in range(1, REACH + 1) for s in (1, -1)]
    for k in steps:
        @pl.when(later(k))
        def _(k=k):
            greet(at_z(k))
        greeted = greeted + jnp.where(later(k), 0, 1)

    @pl.when((d % 4 == 1))
    def _():
        greet((d + 1, r))

    @pl.when((d % 4 == 0) & (d > 0))
    def _():
        greet((d - 1, r))

    greeted = greeted + jnp.where(d % 4 == 2, 1, 0) + jnp.where((d % 4 == 3) & (d < 63), 1, 0)

    w_in = pltpu.make_async_copy(weights.at[0], w_v, load_sem.at[3])
    col_in = pltpu.make_async_copy(columns.at[0], col_s, load_sem.at[4])
    ex_in = pltpu.make_async_copy(excite.at[0], ex_v, load_sem.at[1])
    inv_in = pltpu.make_async_copy(inverse, inv_v, load_sem.at[2])

    @pl.when(source)
    def _():
        ex_in.start()
        inv_in.start()
        fut_in.wait()
        ex_in.wait()
        inv_in.wait()
        right = (ex_v[...].astype(jnp.float32) - fut_v[...]).astype(jnp.bfloat16)
        for k in range(RB):
            got = jnp.dot(inv_v[k], right[k * BLK:(k + 1) * BLK], preferred_element_type=jnp.float32)
            cut = got.astype(jnp.bfloat16).reshape(8, 16, WID)
            if k < 2:
                src_v[pl.ds(k * 8, 8)] = cut
            else:
                half_v[pl.ds(k * 8 - 16, 8)] = cut
            if k == 0:
                whole[0, r] = cut[0]

    w_in.start()
    col_in.start()

    @pl.when(d > 0)
    def _():
        fut_in.wait()
        cast_v[...] = fut_v[...].astype(jnp.bfloat16)

    pl.semaphore_wait(barrier, greeted)

    for k in steps:
        n = wrapped(k)
        sends = (n < 8) | ((n >= 12) & far & (n - z <= 3))
        @pl.when(jnp.logical_not(later(k)) & sends)
        def _(k=k):
            pl.semaphore_signal(ready.at[REACH - k], inc=1, device_id=at_z(k), device_id_type=MESH)

    @pl.when((d % 4 == 3) & (d < 63))
    def _():
        pl.semaphore_signal(ready_shift, inc=1, device_id=(d + 1, r), device_id_type=MESH)

    half_one = remote(half_v.at[0], whole.at[16, r], half_send.at[0], one_recv, partner)
    half_rest = remote(half_v.at[pl.ds(1, 15)], src_v.at[pl.ds(1, 15)], half_send.at[1], half_recv, partner)

    @pl.when(source)
    def _():
        half_rest.start()
        half_one.start()

    def root_one(k):
        return remote(src_v.at[k * 4], whole.at[core * 16 + k * 4, r], one_send.at[k], one_recv, peer_b(k))

    def root_few(k):
        return remote(
            src_v.at[pl.ds(k * 4 + 1, 3)], row_v.at[pl.ds(1, 3)], few_send.at[k], few_recv, peer_b(k)
        )

    def root_own(k):
        return remote(src_v.at[k], whole.at[core * 16 + k, r], one_send.at[3 + k], one_recv, peer_a(k))

    def row_one(k):
        return remote(row_v.at[k], whole.at[core * 16 + b * 4 + k, r], one_send.at[k], one_recv, peer_a(k))

    @pl.when(root & (core == 1))
    def _():
        half_rest.wait_recv()

    @pl.when(root)
    def _():
        for k in (2, 1, 3):
            root_few(k).start()
        for k in (2, 1, 3):
            root_one(k).start()
            root_own(k).start()

    head = near & (a == 0) & (b > 0)

    @pl.when(head)
    def _():
        root_few(1).wait_recv()
        for k in (2, 1, 3):
            row_one(k).start()

    shift_copy = remote(cast_v, shift_v, sh_send, sh_recv, (d - 1, r))

    @pl.when(core == 1)
    def _():
        shift_copy.start()

    @pl.when(near & (d > 0))
    def _():
        root_own(1).wait_recv()

    def line_copy(k):
        return remote(whole.at[mine, r], whole.at[mine, r], line_send.at[REACH + k], line_recv.at[r], at_z(k))

    @pl.when(near)
    def _():
        for k in (4, 3, 2, 1):
            @pl.when(jnp.logical_not(later(-k)))
            def _(k=k):
                line_copy(-k).start()
        for k in (1, 2, 3, 4):
            pl.semaphore_wait(ready.at[REACH + k], 1)
            line_copy(k).start()
        for k in (1, 2, 3, 4):
            @pl.when(later(-k))
            def _(k=k):
                pl.semaphore_wait(ready.at[REACH - k], 1)
                line_copy(-k).start()

    def fwd_copy(k):
        s = z - 4 if k > 0 else (z + 4) % 16
        return remote(
            whole.at[mine, s], whole.at[mine, s], fwd_send.at[REACH + k], line_recv.at[s], at_z(k)
        )

    def got_piece(s):
        remote(whole.at[mine, s], whole.at[mine, s], half_send.at[0], line_recv.at[s], partner).wait_recv()

    def slab(k, m):
        return core * 16 + ((b + 4 - m) % 4) * 4 + (a + 4 - k) % 4

    def other_slab(k, m):
        return (1 - core) * 16 + ((a + 4 - m) % 4) * 4 + (b + 4 - k) % 4

    def part(p, g):
        return whole.at[p]

    def copy_a(g, k):
        here = part(mine, g)
        return remote(here, here, a_send.at[g, k], a_recv.at[g, k], peer_a(k))

    def copy_b(g, k, m):
        here = part(slab(k, 0), g)
        return remote(here, here, b_send.at[g, k, m], b_recv.at[g, k, m], peer_b(m))

    def copy_c(g, k, m):
        here = part(slab(k, m), g)
        return remote(here, here, c_send.at[g, k, m], c_recv.at[g, k, m], partner)

    def got(g, p, sem):
        here = part(p, g)
        remote(here, here, half_send.at[0], sem, partner).wait_recv()

    plus = [((z >= 4) & (z < 8)), ((z >= 8) & (z < 12))]
    minus = [(z >= 12), (z < 4)]
    for h in range(2):
        @pl.when(plus[h])
        def _():
            got_piece(z - 4)
            for k in (1, 2, 3, 4):
                fwd_copy(k).start()

        @pl.when(minus[h])
        def _(h=h):
            got_piece((z + 4) % 16)
            for k in (-1, -2, -3):
                if h == 0:
                    pl.semaphore_wait(ready.at[REACH + k], 1)
                fwd_copy(k).start()

    for g in range(1):
        for s in range(8):
            passed = ((z < 12) & (z - 4 == s)) | (((z >= 12) | (z < 4)) & ((z + 4) % 16 == s))

            @pl.when((far | (r != s)) & jnp.logical_not(passed))
            def _(s=s):
                got_piece(s)

        for k in HOPS:
            copy_a(g, k).start()
        for m in HOPS:
            copy_b(g, 0, m).start()
        copy_c(g, 0, 0).start()

        @pl.when((core == 0) & far)
        def _():
            shift_copy.start()

        @pl.when((core == 0) & near & (d > 0))
        def _():
            pl.semaphore_wait(ready_shift, 1)
            shift_copy.start()

        for k in HOPS:
            got(g, slab(k, 0), a_recv.at[g, k])
            for m in HOPS:
                copy_b(g, k, m).start()
            copy_c(g, k, 0).start()
        for k in (0,) + HOPS:
            for m in HOPS:
                got(g, slab(k, m), b_recv.at[g, k, m])
                copy_c(g, k, m).start()

    w_in.wait()
    col_in.wait()
    for g in range(1):
        for k in (0,) + HOPS:
            for m in (0,) + HOPS:
                got(g, other_slab(k, m), c_recv.at[g, k, m])

    @pl.when(d < 63)
    def _():
        shift_copy.wait_recv()

    @pl.when(d == 63)
    def _():
        shift_v[...] = jnp.zeros_like(shift_v)

    currents[0] = whole[:, r].reshape(ROWS, WID)
    for i in range(RB):
        left = jnp.concatenate([w_v[i, k] for k in range(NNZ)], axis=1)
        picked = []
        for k in range(NNZ):
            j = col_s[i, k]
            picked.append(whole[pl.ds((j % 4) * 8, 8), j // 4].reshape(BLK, WID))
        total = jnp.dot(left, jnp.concatenate(picked, axis=0), preferred_element_type=jnp.float32)
        rows = pl.ds(i * BLK, BLK)
        out[0, rows] = total + shift_v[rows].astype(jnp.float32)

    @pl.when(source)
    def _():
        half_rest.wait_send()
        half_one.wait_send()

    @pl.when(root)
    def _():
        for k in (1, 2, 3):
            root_few(k).wait_send()
            root_one(k).wait_send()
            root_own(k).wait_send()

    @pl.when(head)
    def _():
        for k in (1, 2, 3):
            row_one(k).wait_send()

    @pl.when(d > 0)
    def _():
        shift_copy.wait_send()

    @pl.when(near)
    def _():
        for k in steps:
            line_copy(k).wait_send()

    @pl.when(plus[0] | plus[1])
    def _():
        for k in (1, 2, 3, 4):
            fwd_copy(k).wait_send()

    @pl.when(minus[0] | minus[1])
    def _():
        for k in (-1, -2, -3):
            fwd_copy(k).wait_send()

    for g in range(1):
        for k in HOPS:
            copy_a(g, k).wait_send()
        for k in (0,) + HOPS:
            for m in HOPS:
                copy_b(g, k, m).wait_send()
        for k in (0,) + HOPS:
            for m in (0,) + HOPS:
                copy_c(g, k, m).wait_send()


def write_kernel(currents, out, currents_out, out_out, sem):
    first = pltpu.make_async_copy(out, out_out, sem.at[0])
    second = pltpu.make_async_copy(currents, currents_out, sem.at[1])
    first.start()
    second.start()
    first.wait()
    second.wait()


def per_device(excite, present_inverse, retarded, columns, future_in):
    hbm = pl.BlockSpec(memory_space=pltpu.HBM)
    vmem = pl.BlockSpec(memory_space=pltpu.VMEM)
    dma = pltpu.SemaphoreType.DMA
    flag = pltpu.SemaphoreType.REGULAR
    half, single = jnp.bfloat16, jnp.float32
    results = (
        jax.ShapeDtypeStruct((1, ROWS, WID), half),
        jax.ShapeDtypeStruct((1, ROWS, WID), single),
    )
    held = pl.pallas_call(
        step_kernel,
        out_shape=(pltpu.VMEM((1, ROWS, WID), half), pltpu.VMEM((1, ROWS, WID), single)),
        in_specs=[hbm] * 5,
        out_specs=(vmem, vmem),
        scratch_shapes=[
            pltpu.VMEM((ROWS, WID), half),
            pltpu.VMEM((RB, BLK, BLK), half),
            pltpu.VMEM((RB, NNZ, BLK, BLK), half),
            pltpu.SMEM((RB, NNZ), jnp.int32),
            pltpu.VMEM((ROWS, WID), single),
            pltpu.VMEM((ROWS, WID), half),
            pltpu.VMEM((ROWS, WID), half),
            pltpu.VMEM((16, 16, WID), half),
            pltpu.VMEM((16, 16, WID), half),
            pltpu.VMEM((4, 16, WID), half),
            pltpu.VMEM((32, 8, 16, WID), half),
            dma((5,)), dma((2,)), dma, dma((8,)), dma, dma((4,)), dma,
            dma((9,)), dma((8,)), dma((9,)), flag((9,)), flag,
            dma((1, 4)), dma((1, 4)), dma((1, 4, 4)), dma((1, 4, 4)), dma((1, 4, 4)), dma((1, 4, 4)), dma, dma,
        ],
        compiler_params=pltpu.CompilerParams(collective_id=0, has_side_effects=True, vmem_limit_bytes=56 << 20),
        name="step",
    )(excite, present_inverse, retarded, columns, future_in)
    return pl.pallas_call(
        write_kernel,
        out_shape=results,
        in_specs=[vmem, vmem],
        out_specs=(hbm, hbm),
        scratch_shapes=[dma((2,))],
        compiler_params=pltpu.CompilerParams(vmem_limit_bytes=4 << 20),
        name="write",
    )(*held)


def solution(mesh):
    return jax.shard_map(
        per_device,
        mesh=mesh,
        in_specs=(
            P(None, "row", None),
            P("row", None, None),
            P("delay", "row", None, None, None),
            P("delay", "row", None),
            P("delay", "row", None),
        ),
        out_specs=(P(None, "row", None), P("delay", "row", None)),
        check_vma=False,
    )
```

time: 1180 us -> 41.8 us (0.04)
  waiting for transfers between devices: 1140 us -> 0 us
  Pallas kernels: 0 us -> 41 us
  between operations: 14.1 us -> 0.64 us
    psum x1 -> x0, waiting for transfers between devices: 1080 us -> none  [from_root(): return lax.psum(kept, axis)]
    all_gather x1 -> x0, waiting for transfers between devices: 66.4 us -> none  [per_device(): collected = lax.all_gather(own_rows, 'row', axis=0, tiled=True)]
    pallas_call x0 -> x2, Pallas kernels: none -> 41 us  [the longest x1 40.3 us: per_device(): pl.pallas_call(step_kernel, out_shape=(pltpu.VMEM((1, ROWS, WID), half),...]
  transfers between devices with their start and end apart: 3 -> 0, of which waited for: 2 -> 0; matrix products, arithmetic and copies ran while one was open for 1% -> 0% of each run, Pallas kernels for 0% -> 0%
where the time goes in v2:
time: 41.8 us; the launch traced here: 41.7 us
  Pallas kernels  41 us (98%)
  between operations  0.64 us (2%)
    pallas_call x1, Pallas kernels, per_device(): pl.pallas_call(step_kernel, out_shape=(pltpu.VMEM((1, ROWS, WID), half),...  40.3 us

profile of v2, /device:TPU:1, one launch (start us, length us, event | category | flops | bytes accessed | tf_op | source)
XLA Modules:
  0.0 41.7 jit_solution(2867036694619005606)
XLA Ops:
  0.6 40.3 %step.1 = (bf16[1,512,128]{2,1,0:T(8,128)(2,1)S(1)}, f32[1,512,128]{2,1,0:T(8,128)S(1)}) custom-call(bf16[1,512,128]{2,1,0:T(8,128)(2,1)} %excite.1, bf16[4,128,128]{2,1,0:T(8,128)(2,1)} %inverse.1, bf16[1,4,16,128,128]{4,3,2,1,0:T(8,128)(2,1)} %weights.1, s32[1,4,16]{2,1,0:T(4,128)} %columns.1, f32[1,512,128]{2,1,0:T(8,128)} %future.1), custom_call_target="tpu_custom_call" | custom-call | tf_op jit(solution)/shard_map/step/pallas_call | solution.py:388
  40.9 0.8 %write.1 = (bf16[1,512,128]{2,1,0:T(8,128)(2,1)}, f32[1,512,128]{2,1,0:T(8,128)}) custom-call(bf16[1,512,128]{2,1,0:T(8,128)(2,1)S(1)} %get-tuple-element.4.currents, f32[1,512,128]{2,1,0:T(8,128)S(1)} %get-tuple-element.5.out), custom_call_target="tpu_custom_call" | custom-call | tf_op jit(solution)/shard_map/write/pallas_call | solution.py:412

commit v3 on v2

--- a/solution.py
+++ b/solution.py
@@ -12,15 +12,16 @@
 NNZ = 16
 WID = 128
 HOPS = (1, 3, 2)
+SENDS = (2, 1, 3)
 REACH = 4
 
 
 def step_kernel(
     excite, inverse, weights, columns, future, currents, out,
-    ex_v, inv_v, w_v, col_s, fut_v, cast_v, shift_v, half_v, src_v, row_v, whole,
-    load_sem, half_send, half_recv, one_send, one_recv, few_send, few_recv,
+    ex_v, inv_v, w_v, col_s, fut_v, cast_v, shift_v, pass_v, half_v, src_v, row_v, whole,
+    load_sem, pass_send, pass_recv, half_send, half_recv, one_send, one_recv, few_send, few_recv,
     line_send, line_recv, fwd_send, ready, ready_shift,
-    a_send, a_recv, b_send, b_recv, c_send, c_recv, sh_send, sh_recv,
+    all_send, a_recv, b_recv, c_recv, sh_send, sh_recv,
 ):
     d = lax.axis_index("delay")
     r = lax.axis_index("row")
@@ -84,16 +85,21 @@
         def _(k=k):
             greet(at_z(k))
         greeted = greeted + jnp.where(later(k), 0, 1)
+    for k in (5, 6, 7):
+        @pl.when(z + k < 8)
+        def _(k=k):
+            greet(at_z(k))
+        greeted = greeted + jnp.where(near & (z >= k), 1, 0)
 
     @pl.when((d % 4 == 1))
     def _():
-        greet((d + 1, r))
+        greet((d + 2, r))
 
     @pl.when((d % 4 == 0) & (d > 0))
     def _():
         greet((d - 1, r))
 
-    greeted = greeted + jnp.where(d % 4 == 2, 1, 0) + jnp.where((d % 4 == 3) & (d < 63), 1, 0)
+    greeted = greeted + jnp.where(d % 4 == 3, 1, 0) + jnp.where((d % 4 == 3) & (d < 63), 1, 0)
 
     w_in = pltpu.make_async_copy(weights.at[0], w_v, load_sem.at[3])
     col_in = pltpu.make_async_copy(columns.at[0], col_s, load_sem.at[4])
@@ -139,8 +145,8 @@
     def _():
         pl.semaphore_signal(ready_shift, inc=1, device_id=(d + 1, r), device_id_type=MESH)
 
-    half_one = remote(half_v.at[0], whole.at[16, r], half_send.at[0], one_recv, partner)
-    half_rest = remote(half_v.at[pl.ds(1, 15)], src_v.at[pl.ds(1, 15)], half_send.at[1], half_recv, partner)
+    half_one = remote(half_v.at[0], whole.at[16, r], half_send, one_recv, partner)
+    half_rest = remote(half_v.at[pl.ds(1, 15)], src_v.at[pl.ds(1, 15)], half_send, half_recv, partner)
 
     @pl.when(source)
     def _():
@@ -148,18 +154,18 @@
         half_one.start()
 
     def root_one(k):
-        return remote(src_v.at[k * 4], whole.at[core * 16 + k * 4, r], one_send.at[k], one_recv, peer_b(k))
+        return remote(src_v.at[k * 4], whole.at[core * 16 + k * 4, r], one_send, one_recv, peer_b(k))
 
     def root_few(k):
         return remote(
-            src_v.at[pl.ds(k * 4 + 1, 3)], row_v.at[pl.ds(1, 3)], few_send.at[k], few_recv, peer_b(k)
+            src_v.at[pl.ds(k * 4 + 1, 3)], row_v.at[pl.ds(1, 3)], few_send, few_recv, peer_b(k)
         )
 
     def root_own(k):
-        return remote(src_v.at[k], whole.at[core * 16 + k, r], one_send.at[3 + k], one_recv, peer_a(k))
+        return remote(src_v.at[k], whole.at[core * 16 + k, r], one_send, one_recv, peer_a(k))
 
     def row_one(k):
-        return remote(row_v.at[k], whole.at[core * 16 + b * 4 + k, r], one_send.at[k], one_recv, peer_a(k))
+        return remote(row_v.at[k], whole.at[core * 16 + b * 4 + k, r], one_send, one_recv, peer_a(k))
 
     @pl.when(root & (core == 1))
     def _():
@@ -183,21 +189,28 @@
 
     shift_copy = remote(cast_v, shift_v, sh_send, sh_recv, (d - 1, r))
 
+    handed = remote(cast_v, pass_v, pass_send, pass_recv, partner)
+    passed_on = remote(pass_v, shift_v, pass_send, sh_recv, (d - 2, r))
+
     @pl.when(core == 1)
     def _():
         shift_copy.start()
 
+    @pl.when(far & (core == 0))
+    def _():
+        handed.start()
+
     @pl.when(near & (d > 0))
     def _():
         root_own(1).wait_recv()
 
     def line_copy(k):
-        return remote(whole.at[mine, r], whole.at[mine, r], line_send.at[REACH + k], line_recv.at[r], at_z(k))
+        return remote(whole.at[mine, r], whole.at[mine, r], line_send, line_recv.at[r], at_z(k))
 
     @pl.when(near)
     def _():
-        for k in (4, 3, 2, 1):
-            @pl.when(jnp.logical_not(later(-k)))
+        for k in (7, 6, 5, 4, 3, 2, 1):
+            @pl.when(z >= k)
             def _(k=k):
                 line_copy(-k).start()
         for k in (1, 2, 3, 4):
@@ -212,93 +225,138 @@
     def fwd_copy(k):
         s = z - 4 if k > 0 else (z + 4) % 16
         return remote(
-            whole.at[mine, s], whole.at[mine, s], fwd_send.at[REACH + k], line_recv.at[s], at_z(k)
+            whole.at[mine, s], whole.at[mine, s], fwd_send, line_recv.at[s], at_z(k)
         )
 
     def got_piece(s):
-        remote(whole.at[mine, s], whole.at[mine, s], half_send.at[0], line_recv.at[s], partner).wait_recv()
-
-    def slab(k, m):
-        return core * 16 + ((b + 4 - m) % 4) * 4 + (a + 4 - k) % 4
-
-    def other_slab(k, m):
-        return (1 - core) * 16 + ((a + 4 - m) % 4) * 4 + (b + 4 - k) % 4
+        remote(whole.at[mine, s], whole.at[mine, s], half_send, line_recv.at[s], partner).wait_recv()
+
+    def slab(k):
+        return core * 16 + b * 4 + (a + 4 - k) % 4
 
     def part(p, g):
-        return whole.at[p]
+        return whole.at[p, pl.ds(g * 4, 4)]
+
+    def lane(m, g):
+        return whole.at[pl.ds(core * 16 + ((b + 4 - m) % 4) * 4, 4), pl.ds(g * 4, 4)]
 
     def copy_a(g, k):
         here = part(mine, g)
-        return remote(here, here, a_send.at[g, k], a_recv.at[g, k], peer_a(k))
+        return remote(here, here, all_send, a_recv.at[g, k - 1], peer_a(k))
 
     def copy_b(g, k, m):
-        here = part(slab(k, 0), g)
-        return remote(here, here, b_send.at[g, k, m], b_recv.at[g, k, m], peer_b(m))
-
-    def copy_c(g, k, m):
-        here = part(slab(k, m), g)
-        return remote(here, here, c_send.at[g, k, m], c_recv.at[g, k, m], partner)
-
-    def got(g, p, sem):
-        here = part(p, g)
-        remote(here, here, half_send.at[0], sem, partner).wait_recv()
+        here = part(slab(k), g)
+        return remote(here, here, all_send, b_recv.at[g, m - 1], peer_b(m))
+
+    def copy_c(g, m):
+        here = lane(m, g)
+        return remote(here, here, all_send, c_recv, partner)
 
     plus = [((z >= 4) & (z < 8)), ((z >= 8) & (z < 12))]
     minus = [(z >= 12), (z < 4)]
-    for h in range(2):
+    def forward_up(h):
         @pl.when(plus[h])
         def _():
             got_piece(z - 4)
-            for k in (1, 2, 3, 4):
+            for k in (4, 3, 2, 1):
                 fwd_copy(k).start()
 
+    def forward_down(h):
         @pl.when(minus[h])
-        def _(h=h):
+        def _():
             got_piece((z + 4) % 16)
-            for k in (-1, -2, -3):
+            for k in (-3, -2, -1):
                 if h == 0:
                     pl.semaphore_wait(ready.at[REACH + k], 1)
-                fwd_copy(k).start()
-
-    for g in range(1):
-        for s in range(8):
-            passed = ((z < 12) & (z - 4 == s)) | (((z >= 12) | (z < 4)) & ((z + 4) % 16 == s))
+                    fwd_copy(k).start()
+                else:
+                    @pl.when(z + k < 0)
+                    def _(k=k):
+                        fwd_copy(k).start()
+
+    def pieces(g):
+        for s in range(g * 4, g * 4 + 4):
+            passed = (plus[g] & (z - 4 == s)) | (minus[g] & ((z + 4) % 16 == s))
 
             @pl.when((far | (r != s)) & jnp.logical_not(passed))
             def _(s=s):
                 got_piece(s)
 
+    def spread(g):
+        for k in SENDS:
+            copy_a(g, k).start()
+        for m in SENDS:
+            copy_b(g, 0, m).start()
+
+    def pass_on(g):
         for k in HOPS:
-            copy_a(g, k).start()
+            copy_a(g, k).wait_recv()
+            for m in SENDS:
+                copy_b(g, k, m).start()
+        copy_c(g, 0).start()
+
+    def share(g):
         for m in HOPS:
-            copy_b(g, 0, m).start()
-        copy_c(g, 0, 0).start()
-
-        @pl.when((core == 0) & far)
-        def _():
-            shift_copy.start()
-
-        @pl.when((core == 0) & near & (d > 0))
-        def _():
-            pl.semaphore_wait(ready_shift, 1)
-            shift_copy.start()
-
-        for k in HOPS:
-            got(g, slab(k, 0), a_recv.at[g, k])
-            for m in HOPS:
-                copy_b(g, k, m).start()
-            copy_c(g, k, 0).start()
-        for k in (0,) + HOPS:
-            for m in HOPS:
-                got(g, slab(k, m), b_recv.at[g, k, m])
-                copy_c(g, k, m).start()
+            here = lane(m, g)
+            remote(here, here, all_send, b_recv.at[g, m - 1], partner).wait_recv()
+            copy_c(g, m).start()
+
+    forward_up(0)
+    forward_down(0)
+    forward_up(1)
+
+    @pl.when(far & (core == 1))
+    def _():
+        handed.wait_recv()
+        passed_on.start()
+
+    pieces(0)
+    spread(0)
+    forward_down(1)
+    pass_on(0)
+    pieces(1)
+    spread(1)
+
+    share(0)
+    pass_on(1)
+
+    @pl.when((core == 0) & near & (d > 0))
+    def _():
+        pl.semaphore_wait(ready_shift, 1)
+        shift_copy.start()
+
+    share(1)
+
+    def drained(src, sem):
+        remote(src, src, sem, c_recv, partner).wait_send()
+
+    @pl.when(source)
+    def _():
+        drained(src_v, half_send)
+
+    @pl.when(root)
+    def _():
+        drained(src_v.at[pl.ds(0, 9)], few_send)
+        drained(src_v.at[pl.ds(0, 6)], one_send)
+
+    @pl.when(head)
+    def _():
+        drained(src_v.at[pl.ds(0, 3)], one_send)
+
+    for low, high, count in ((0, 4, 8), (5, 5, 9), (6, 6, 10), (7, 7, 11)):
+        @pl.when((z >= low) & (z <= high))
+        def _(count=count):
+            drained(src_v.at[pl.ds(0, count)], line_send)
+
+    for low, high, count in ((0, 0, 3), (1, 1, 2), (2, 2, 1), (4, 11, 4), (12, 15, 3)):
+        @pl.when((z >= low) & (z <= high))
+        def _(count=count):
+            drained(src_v.at[pl.ds(0, count)], fwd_send)
 
     w_in.wait()
     col_in.wait()
-    for g in range(1):
-        for k in (0,) + HOPS:
-            for m in (0,) + HOPS:
-                got(g, other_slab(k, m), c_recv.at[g, k, m])
+    there = whole.at[pl.ds(0, 16)]
+    remote(there, there, all_send, c_recv, partner).wait_recv()
 
     @pl.when(d < 63)
     def _():
@@ -319,51 +377,19 @@
         rows = pl.ds(i * BLK, BLK)
         out[0, rows] = total + shift_v[rows].astype(jnp.float32)
 
-    @pl.when(source)
-    def _():
-        half_rest.wait_send()
-        half_one.wait_send()
-
-    @pl.when(root)
-    def _():
-        for k in (1, 2, 3):
-            root_few(k).wait_send()
-            root_one(k).wait_send()
-            root_own(k).wait_send()
-
-    @pl.when(head)
-    def _():
-        for k in (1, 2, 3):
-            row_one(k).wait_send()
-
-    @pl.when(d > 0)
+    drained(whole.at[pl.ds(0, 31)], all_send)
+
+    @pl.when((d > 0) & (near | (core == 1)))
     def _():
         shift_copy.wait_send()
 
-    @pl.when(near)
-    def _():
-        for k in steps:
-            line_copy(k).wait_send()
-
-    @pl.when(plus[0] | plus[1])
-    def _():
-        for k in (1, 2, 3, 4):
-            fwd_copy(k).wait_send()
-
-    @pl.when(minus[0] | minus[1])
-    def _():
-        for k in (-1, -2, -3):
-            fwd_copy(k).wait_send()
-
-    for g in range(1):
-        for k in HOPS:
-            copy_a(g, k).wait_send()
-        for k in (0,) + HOPS:
-            for m in HOPS:
-                copy_b(g, k, m).wait_send()
-        for k in (0,) + HOPS:
-            for m in (0,) + HOPS:
-                copy_c(g, k, m).wait_send()
+    @pl.when(far & (core == 0))
+    def _():
+        handed.wait_send()
+
+    @pl.when(far & (core == 1))
+    def _():
+        passed_on.wait_send()
 
 
 def write_kernel(currents, out, currents_out, out_out, sem):
@@ -376,7 +402,7 @@
 
 
 def per_device(excite, present_inverse, retarded, columns, future_in):
-    hbm = pl.BlockSpec(memory_space=pltpu.HBM)
+    hbm = pl.BlockSpec(memory_space=pl.ANY)
     vmem = pl.BlockSpec(memory_space=pltpu.VMEM)
     dma = pltpu.SemaphoreType.DMA
     flag = pltpu.SemaphoreType.REGULAR
@@ -398,13 +424,14 @@
             pltpu.VMEM((ROWS, WID), single),
             pltpu.VMEM((ROWS, WID), half),
             pltpu.VMEM((ROWS, WID), half),
+            pltpu.VMEM((ROWS, WID), half),
             pltpu.VMEM((16, 16, WID), half),
             pltpu.VMEM((16, 16, WID), half),
             pltpu.VMEM((4, 16, WID), half),
             pltpu.VMEM((32, 8, 16, WID), half),
-            dma((5,)), dma((2,)), dma, dma((8,)), dma, dma((4,)), dma,
-            dma((9,)), dma((8,)), dma((9,)), flag((9,)), flag,
-            dma((1, 4)), dma((1, 4)), dma((1, 4, 4)), dma((1, 4, 4)), dma((1, 4, 4)), dma((1, 4, 4)), dma, dma,
+            dma((5,)), dma, dma, dma, dma, dma, dma, dma, dma,
+            dma, dma((8,)), dma, flag((9,)), flag,
+            dma, dma((2, 3)), dma((2, 3)), dma, dma, dma,
         ],
         compiler_params=pltpu.CompilerParams(collective_id=0, has_side_effects=True, vmem_limit_bytes=56 << 20),
         name="step",

time: 41.8 us -> 36 us (0.86)
  Pallas kernels: 41 us -> 35.2 us
    pallas_call x1, Pallas kernels: 40.3 us -> 34.5 us  [per_device(): pl.pallas_call(step_kernel, out_shape=(pltpu.VMEM((1, ROWS, WID), half),...]
where the time goes in v3:
time: 36 us; the launch traced here: 35.9 us
  Pallas kernels  35.2 us (98%)
  between operations  0.64 us (2%)
    pallas_call x1, Pallas kernels, per_device(): pl.pallas_call(step_kernel, out_shape=(pltpu.VMEM((1, ROWS, WID), half),...  34.5 us
    pallas_call x1, Pallas kernels, per_device(): pl.pallas_call(write_kernel, out_shape=results, in_specs=[vmem, vmem], ou...  0.76 us

profile of v3, /device:TPU:1, one launch (start us, length us, event | category | flops | bytes accessed | tf_op | source)
XLA Modules:
  0.0 35.9 jit_solution(3441372630029039548)
XLA Ops:
  0.6 34.5 %step.1 = (bf16[1,512,128]{2,1,0:T(8,128)(2,1)S(1)}, f32[1,512,128]{2,1,0:T(8,128)S(1)}) custom-call(bf16[1,512,128]{2,1,0:T(8,128)(2,1)} %excite.1, bf16[4,128,128]{2,1,0:T(8,128)(2,1)} %inverse.1, bf16[1,4,16,128,128]{4,3,2,1,0:T(8,128)(2,1)} %weights.1, s32[1,4,16]{2,1,0:T(4,128)} %columns.1, f32[1,512,128]{2,1,0:T(8,128)} %future.1), custom_call_target="tpu_custom_call" | custom-call | tf_op jit(solution)/shard_map/step/pallas_call | solution.py:414
  35.1 0.8 %write.1 = (bf16[1,512,128]{2,1,0:T(8,128)(2,1)}, f32[1,512,128]{2,1,0:T(8,128)}) custom-call(bf16[1,512,128]{2,1,0:T(8,128)(2,1)S(1)} %get-tuple-element.4.currents, f32[1,512,128]{2,1,0:T(8,128)S(1)} %get-tuple-element.5.out), custom_call_target="tpu_custom_call" | custom-call | tf_op jit(solution)/shard_map/write/pallas_call | solution.py:439

commit v4 on v3

--- a/solution.py
+++ b/solution.py
@@ -13,6 +13,7 @@
 WID = 128
 HOPS = (1, 3, 2)
 SENDS = (2, 1, 3)
+ORDER = sorted(range(32), key=lambda p: -(min((p // 4) % 4, 4 - (p // 4) % 4) + min(p % 4, 4 - p % 4)))
 REACH = 4
 
 
@@ -21,7 +22,7 @@
     ex_v, inv_v, w_v, col_s, fut_v, cast_v, shift_v, pass_v, half_v, src_v, row_v, whole,
     load_sem, pass_send, pass_recv, half_send, half_recv, one_send, one_recv, few_send, few_recv,
     line_send, line_recv, fwd_send, ready, ready_shift,
-    all_send, a_recv, b_recv, c_recv, sh_send, sh_recv,
+    all_send, direct_send, a_recv, b_recv, c_recv, sh_send, sh_recv,
 ):
     d = lax.axis_index("delay")
     r = lax.axis_index("row")
@@ -85,11 +86,16 @@
         def _(k=k):
             greet(at_z(k))
         greeted = greeted + jnp.where(later(k), 0, 1)
-    for k in (5, 6, 7):
-        @pl.when(z + k < 8)
+    for k in (5, 6):
+        @pl.when((z + k < 8) & (z >= k - 5))
         def _(k=k):
             greet(at_z(k))
-        greeted = greeted + jnp.where(near & (z >= k), 1, 0)
+        greeted = greeted + jnp.where(near & (z >= k + k % 5), 1, 0)
+    @pl.when(z == 0)
+    def _():
+        greet((0, 7))
+        greet((0, 6))
+    greeted = greeted + jnp.where(source & (r >= 6), 32, 0)
 
     @pl.when((d % 4 == 1))
     def _():
@@ -179,6 +185,16 @@
             root_one(k).start()
             root_own(k).start()
 
+    @pl.when(source & (r >= 6))
+    def _():
+        for p in ORDER:
+            pc, pb, pa = p // 16, (p // 4) % 4, p % 4
+            px, py = (pb, pa) if pc else (pa, pb)
+            remote(
+                half_v.at[p - 16] if pc else src_v.at[p], whole.at[p, r], direct_send, line_recv.at[r],
+                ((py * 4 + px) * 4 + pc, 0),
+            ).start()
+
     head = near & (a == 0) & (b > 0)
 
     @pl.when(head)
@@ -209,8 +225,8 @@
 
     @pl.when(near)
     def _():
-        for k in (7, 6, 5, 4, 3, 2, 1):
-            @pl.when(z >= k)
+        for k in (6, 5, 4, 3, 2, 1):
+            @pl.when(z >= k + k // 6)
             def _(k=k):
                 line_copy(-k).start()
         for k in (1, 2, 3, 4):
@@ -317,14 +333,15 @@
     pieces(1)
     spread(1)
 
+    @pl.when((core == 0) & near & (d > 0))
+    def _():
+        pl.semaphore_wait(ready_shift, 1)
+        shift_copy.start()
+
+
     share(0)
     pass_on(1)
 
-    @pl.when((core == 0) & near & (d > 0))
-    def _():
-        pl.semaphore_wait(ready_shift, 1)
-        shift_copy.start()
-
     share(1)
 
     def drained(src, sem):
@@ -334,6 +351,10 @@
     def _():
         drained(src_v, half_send)
 
+    @pl.when(source & (r >= 6))
+    def _():
+        drained(whole.at[pl.ds(0, 4)], direct_send)
+
     @pl.when(root)
     def _():
         drained(src_v.at[pl.ds(0, 9)], few_send)
@@ -343,7 +364,7 @@
     def _():
         drained(src_v.at[pl.ds(0, 3)], one_send)
 
-    for low, high, count in ((0, 4, 8), (5, 5, 9), (6, 6, 10), (7, 7, 11)):
+    for low, high, count in ((0, 4, 8), (5, 6, 9), (7, 7, 10)):
         @pl.when((z >= low) & (z <= high))
         def _(count=count):
             drained(src_v.at[pl.ds(0, count)], line_send)
@@ -431,7 +452,7 @@
             pltpu.VMEM((32, 8, 16, WID), half),
             dma((5,)), dma, dma, dma, dma, dma, dma, dma, dma,
             dma, dma((8,)), dma, flag((9,)), flag,
-            dma, dma((2, 3)), dma((2, 3)), dma, dma, dma,
+            dma, dma, dma((2, 3)), dma((2, 3)), dma, dma, dma,
         ],
         compiler_params=pltpu.CompilerParams(collective_id=0, has_side_effects=True, vmem_limit_bytes=56 << 20),
         name="step",

time: 36 us -> 34.9 us (0.969)
  Pallas kernels: 35.2 us -> 34.1 us
    pallas_call x1, Pallas kernels: 34.5 us -> 33.4 us  [per_device(): pl.pallas_call(step_kernel, out_shape=(pltpu.VMEM((1, ROWS, WID), half),...]
where the time goes in v4:
time: 34.9 us; the launch traced here: 34.8 us
  Pallas kernels  34.1 us (98%)
  between operations  0.64 us (2%)
    pallas_call x1, Pallas kernels, per_device(): pl.pallas_call(step_kernel, out_shape=(pltpu.VMEM((1, ROWS, WID), half),...  33.4 us
    pallas_call x1, Pallas kernels, per_device(): pl.pallas_call(write_kernel, out_shape=results, in_specs=[vmem, vmem], ou...  0.76 us

profile of v4, /device:TPU:1, one launch (start us, length us, event | category | flops | bytes accessed | tf_op | source)
XLA Modules:
  0.0 34.8 jit_solution(16788531149481551359)
XLA Ops:
  0.6 33.4 %step.1 = (bf16[1,512,128]{2,1,0:T(8,128)(2,1)S(1)}, f32[1,512,128]{2,1,0:T(8,128)S(1)}) custom-call(bf16[1,512,128]{2,1,0:T(8,128)(2,1)} %excite.1, bf16[4,128,128]{2,1,0:T(8,128)(2,1)} %inverse.1, bf16[1,4,16,128,128]{4,3,2,1,0:T(8,128)(2,1)} %weights.1, s32[1,4,16]{2,1,0:T(4,128)} %columns.1, f32[1,512,128]{2,1,0:T(8,128)} %future.1), custom_call_target="tpu_custom_call" | custom-call | tf_op jit(solution)/shard_map/step/pallas_call | solution.py:435
  34.0 0.8 %write.1 = (bf16[1,512,128]{2,1,0:T(8,128)(2,1)}, f32[1,512,128]{2,1,0:T(8,128)}) custom-call(bf16[1,512,128]{2,1,0:T(8,128)(2,1)S(1)} %get-tuple-element.4.currents, f32[1,512,128]{2,1,0:T(8,128)S(1)} %get-tuple-element.5.out), custom_call_target="tpu_custom_call" | custom-call | tf_op jit(solution)/shard_map/write/pallas_call | solution.py:460

commit v5 on v4

--- a/solution.py
+++ b/solution.py
@@ -87,15 +87,15 @@
             greet(at_z(k))
         greeted = greeted + jnp.where(later(k), 0, 1)
     for k in (5, 6):
-        @pl.when((z + k < 8) & (z >= k - 5))
+        @pl.when((z + k < 8) & (z > 0))
         def _(k=k):
             greet(at_z(k))
-        greeted = greeted + jnp.where(near & (z >= k + k % 5), 1, 0)
+        greeted = greeted + jnp.where(near & (z > k), 1, 0)
     @pl.when(z == 0)
     def _():
-        greet((0, 7))
-        greet((0, 6))
-    greeted = greeted + jnp.where(source & (r >= 6), 32, 0)
+        for k in range(1, 8):
+            greet((0, k))
+    greeted = greeted + jnp.where(source & (r > 0), 32, 0)
 
     @pl.when((d % 4 == 1))
     def _():
@@ -185,7 +185,7 @@
             root_one(k).start()
             root_own(k).start()
 
-    @pl.when(source & (r >= 6))
+    @pl.when(source & (r > 0))
     def _():
         for p in ORDER:
             pc, pb, pa = p // 16, (p // 4) % 4, p % 4
@@ -226,14 +226,14 @@
     @pl.when(near)
     def _():
         for k in (6, 5, 4, 3, 2, 1):
-            @pl.when(z >= k + k // 6)
+            @pl.when(z > k)
             def _(k=k):
                 line_copy(-k).start()
         for k in (1, 2, 3, 4):
             pl.semaphore_wait(ready.at[REACH + k], 1)
             line_copy(k).start()
         for k in (1, 2, 3, 4):
-            @pl.when(later(-k))
+            @pl.when(later(-k) & (z > 0))
             def _(k=k):
                 pl.semaphore_wait(ready.at[REACH - k], 1)
                 line_copy(-k).start()
@@ -269,7 +269,7 @@
         return remote(here, here, all_send, c_recv, partner)
 
     plus = [((z >= 4) & (z < 8)), ((z >= 8) & (z < 12))]
-    minus = [(z >= 12), (z < 4)]
+    minus = [(z >= 12), (z < 0), (z < 4)]
     def forward_up(h):
         @pl.when(plus[h])
         def _():
@@ -292,7 +292,7 @@
 
     def pieces(g):
         for s in range(g * 4, g * 4 + 4):
-            passed = (plus[g] & (z - 4 == s)) | (minus[g] & ((z + 4) % 16 == s))
+            passed = (plus[g] & (z - 4 == s)) | ((minus[g] | minus[2]) & ((z + 4) % 16 == s))
 
             @pl.when((far | (r != s)) & jnp.logical_not(passed))
             def _(s=s):
@@ -328,8 +328,15 @@
 
     pieces(0)
     spread(0)
-    forward_down(1)
+
+    @pl.when(z == 0)
+    def _():
+        for k in (1, 2, 3, 4):
+            pl.semaphore_wait(ready.at[REACH - k], 1)
+            line_copy(-k).start()
+
     pass_on(0)
+    forward_down(2)
     pieces(1)
     spread(1)
 
@@ -351,7 +358,7 @@
     def _():
         drained(src_v, half_send)
 
-    @pl.when(source & (r >= 6))
+    @pl.when(source & (r > 0))
     def _():
         drained(whole.at[pl.ds(0, 4)], direct_send)
 
@@ -364,7 +371,7 @@
     def _():
         drained(src_v.at[pl.ds(0, 3)], one_send)
 
-    for low, high, count in ((0, 4, 8), (5, 6, 9), (7, 7, 10)):
+    for low, high, count in ((0, 0, 8), (1, 4, 7), (5, 5, 8), (6, 6, 9), (7, 7, 10)):
         @pl.when((z >= low) & (z <= high))
         def _(count=count):
             drained(src_v.at[pl.ds(0, count)], line_send)

time: 34.9 us -> 33.9 us (0.971)
  the two profiles are of different devices: /device:TPU:1 before, /device:TPU:33 now
where the time goes in v5:
time: 33.9 us; the launch traced here: 33.7 us
  Pallas kernels  33.1 us (98%)
  between operations  0.64 us (2%)
    pallas_call x1, Pallas kernels, per_device(): pl.pallas_call(step_kernel, out_shape=(pltpu.VMEM((1, ROWS, WID), half),...  32.3 us
    pallas_call x1, Pallas kernels, per_device(): pl.pallas_call(write_kernel, out_shape=results, in_specs=[vmem, vmem], ou...  0.76 us

profile of v5, /device:TPU:33, one launch (start us, length us, event | category | flops | bytes accessed | tf_op | source)
XLA Modules:
  0.0 33.7 jit_solution(6150246957278632662)
XLA Ops:
  0.6 32.3 %step.1 = (bf16[1,512,128]{2,1,0:T(8,128)(2,1)S(1)}, f32[1,512,128]{2,1,0:T(8,128)S(1)}) custom-call(bf16[1,512,128]{2,1,0:T(8,128)(2,1)} %excite.1, bf16[4,128,128]{2,1,0:T(8,128)(2,1)} %inverse.1, bf16[1,4,16,128,128]{4,3,2,1,0:T(8,128)(2,1)} %weights.1, s32[1,4,16]{2,1,0:T(4,128)} %columns.1, f32[1,512,128]{2,1,0:T(8,128)} %future.1), custom_call_target="tpu_custom_call" | custom-call | tf_op jit(solution)/shard_map/step/pallas_call | solution.py:442
  32.9 0.8 %write.1 = (bf16[1,512,128]{2,1,0:T(8,128)(2,1)}, f32[1,512,128]{2,1,0:T(8,128)}) custom-call(bf16[1,512,128]{2,1,0:T(8,128)(2,1)S(1)} %get-tuple-element.4.currents, f32[1,512,128]{2,1,0:T(8,128)S(1)} %get-tuple-element.5.out), custom_call_target="tpu_custom_call" | custom-call | tf_op jit(solution)/shard_map/write/pallas_call | solution.py:467
